TPU v7x, 32 devices: a whole 2x2x4 slice. The times are simulated.
32 devices in a mesh: rep: 8 (over z, x), grp: 4 (over y, core).
Axes of the slice: x: 2, y: 2, z: 4, core: 2. Of those that a mesh axis runs over, the one named last changes fastest.
Arguments:
- images: bfloat16 [32, 14, 14, 512], P(('rep', 'grp')), may hold values from -45 to 45
- cotangent: bfloat16 [32, 14, 14, 512], P(('rep', 'grp')), may hold values from -6 to 6
- region_ids: int32 [14, 14], replicated, may hold values from 0 to 8, as said below
- rel_index: int32 [169], replicated, may hold values from 0 to 168, each once
- matrices: float32 [3145728], P(('rep', 'grp')), may hold values from -0.8838835 to 0.8838835
- matrix_m: float32 [3145728], P(('rep', 'grp')), may hold values from -0.75 to 0.75
- matrix_v: float32 [3145728], P(('rep', 'grp')), may hold values from 2e-05 to 0.0005
- small: float32 [8848], replicated, may hold values from -4 to 301.5
- small_m: float32 [8848], replicated, may hold values from -0.75 to 0.75
- small_v: float32 [8848], replicated, may hold values from 2e-05 to 0.0005
Outputs:
- output: bfloat16 [32, 14, 14, 512], P(('rep', 'grp'))
- input_grad: bfloat16 [32, 14, 14, 512], P(('rep', 'grp'))
- matrix_grad: float32 [3145728], P(('rep', 'grp'))
- small_grad: float32 [8848], replicated
- new_matrices: float32 [3145728], P(('rep', 'grp'))
- new_matrix_m: float32 [3145728], P(('rep', 'grp'))
- new_matrix_v: float32 [3145728], P(('rep', 'grp'))
- new_small: float32 [8848], replicated
- new_small_m: float32 [8848], replicated
- new_small_v: float32 [8848], replicated
Inputs may be any that keep to these rules, and one draw needn't show every extreme that they name: `region_ids`: 3 times a row band plus a column band; each dimension is cut into three nonempty bands. `rel_index`: a permutation of the table's rows.
All inputs are finite; a program needn't handle non-finite values.
Results may differ from a plain program's by a relative error of at most 0.01.
The roundings to bfloat16 on the way count: a program that leaves them out, or rounds other values in their place, can miss the bound.
Values may be sent and summed in bfloat16 or wider, within the bound.
No kernel may reach another device: no remote copies, remote signals or barrier semaphores. Data moves between devices by JAX's collectives and lax.ppermute only.
A program may use at most 128 MiB of HBM per device.

v0:
```python
import math
import jax
import jax.numpy as jnp
from jax import lax
from jax.sharding import PartitionSpec as P

D = 512
HEADS = 16
FF = 2048
WIN = 7
SIDE = 14
SHIFT = 3
STEP = 5
HEAD_DIM = 32
REL = 169
norm_eps = 1e-05
beta_one = 0.9
beta_two = 0.999
adam_eps = 1e-08
rate_matrix = 0.01
rate_small = 0.2
decay_rate = 0.05
masked_score = -1e30
root_half = 0.7071067811865476
inv_root_twopi = 0.3989422804014327
highest = lax.Precision.HIGHEST


def norm_stats(values):
    center = values - jnp.mean(values, axis=-1, keepdims=True)
    spread = jnp.mean(center * center, axis=-1, keepdims=True)
    scaling = lax.rsqrt(spread + norm_eps)
    return (center * scaling, scaling)


def norm_back(incoming, normed, scaling, gain_vector):
    scaled = incoming * gain_vector
    backward = scaling * (
        scaled
        - jnp.mean(scaled, axis=-1, keepdims=True)
        - normed * jnp.mean(scaled * normed, axis=-1, keepdims=True)
    )
    return (backward, jnp.sum(incoming * normed, axis=(0, 1, 2)), jnp.sum(incoming, axis=(0, 1, 2)))


def gelu_slope(values):
    return (
        0.5 * (1.0 + lax.erf(values * root_half))
        + values * jnp.exp(-0.5 * values * values) * inv_root_twopi
    )


def to_windows(spatial):
    image_count = spatial.shape[0]
    blocks = SIDE // WIN
    rolled = jnp.roll(spatial, (-SHIFT, -SHIFT), axis=(1, 2))
    blocked = rolled.reshape(image_count, blocks, WIN, blocks, WIN, spatial.shape[-1])
    return blocked.transpose(0, 1, 3, 2, 4, 5).reshape(
        image_count, blocks * blocks, WIN * WIN, spatial.shape[-1]
    )


def from_windows(window_grid):
    image_count = window_grid.shape[0]
    blocks = SIDE // WIN
    blocked = window_grid.reshape(image_count, blocks, blocks, WIN, WIN, window_grid.shape[-1])
    spatial = blocked.transpose(0, 1, 3, 2, 4, 5).reshape(
        image_count, SIDE, SIDE, window_grid.shape[-1]
    )
    return jnp.roll(spatial, (SHIFT, SHIFT), axis=(1, 2))


def allowed_pairs(region_ids):
    blocks = SIDE // WIN
    window_grid = (
        region_ids.reshape(blocks, WIN, blocks, WIN)
        .transpose(0, 2, 1, 3)
        .reshape(blocks * blocks, WIN * WIN)
    )
    return window_grid[:, :, None] == window_grid[:, None, :]


def offset_grid():
    spots = jnp.arange(WIN * WIN, dtype=jnp.int32)
    rows_at = spots // WIN
    cols_at = spots % WIN
    return (rows_at[:, None] - rows_at[None, :] + WIN - 1) * (2 * WIN - 1) + (
        cols_at[:, None] - cols_at[None, :] + WIN - 1
    )


def lookup_tables(rel_index):
    labels = jnp.arange(REL, dtype=jnp.int32)
    select_offset = (offset_grid().reshape(-1)[:, None] == labels[None, :]).astype(jnp.float32)
    select_row = (rel_index[:, None] == labels[None, :]).astype(jnp.float32)
    return (select_offset, select_row)


def unpack_matrices(flat_weights):
    bound_one = 3 * D * D
    bound_two = bound_one + D * D
    bound_three = bound_two + D * FF
    return (
        flat_weights[:bound_one].reshape(D, 3 * D),
        flat_weights[bound_one:bound_two].reshape(D, D),
        flat_weights[bound_two:bound_three].reshape(D, FF),
        flat_weights[bound_three:].reshape(FF, D),
    )


def unpack_small(small):
    pieces = [small[number * D : (number + 1) * D] for number in range(8)]
    bias_up = small[8 * D : 8 * D + FF]
    rel_table = small[8 * D + FF :].reshape(REL, HEADS)
    return pieces + [bias_up, rel_table]


def adam_step(weights, first_moment, second_moment, gradient, rate, decay):
    new_first = beta_one * first_moment + (1.0 - beta_one) * gradient
    new_second = beta_two * second_moment + (1.0 - beta_two) * gradient * gradient
    first_hat = new_first / (1.0 - beta_one**STEP)
    second_hat = new_second / (1.0 - beta_two**STEP)
    update = first_hat / (jnp.sqrt(second_hat) + adam_eps) + decay * weights
    return (weights - rate * update, new_first, new_second)


def on_device(
    images, cotangent, region_ids, rel_index, matrices, matrix_m, matrix_v, small, small_m, small_v
):
    low_shard = matrices.astype(jnp.bfloat16)
    gathered = lax.all_gather(low_shard, ("rep", "grp"), axis=0, tiled=True)
    weight_qkv, weight_proj, weight_up, weight_down = unpack_matrices(gathered)
    small_parts = unpack_small(small)
    gain_one, gain_two, shift_one, bias_query, bias_value, bias_proj, shift_two, bias_down = (
        small_parts[:8]
    )
    bias_up = small_parts[8]
    image_count = images.shape[0]
    row_count = image_count * SIDE * SIDE
    places = WIN * WIN
    windows_count = (SIDE // WIN) ** 2
    score_scale = HEAD_DIM ** (-0.5)
    allowed = allowed_pairs(region_ids)[None, :, None]
    select_offset, select_row = lookup_tables(rel_index)
    table_rows = jnp.dot(select_row, small_parts[9], precision=highest)
    rel_bias = (
        jnp.dot(select_offset, table_rows, precision=highest)
        .reshape(places, places, HEADS)
        .transpose(2, 0, 1)
    )
    image_values = images.astype(jnp.float32)
    normed_one, scaling_one = norm_stats(image_values)
    input_one = (normed_one * gain_one + shift_one).astype(jnp.bfloat16)
    window_rows = to_windows(input_one).reshape(row_count, D)
    zeros_key = jnp.zeros((D,), jnp.float32)
    projected = jnp.dot(
        window_rows, weight_qkv, preferred_element_type=jnp.float32
    ) + jnp.concatenate([bias_query, zeros_key, bias_value])
    projected = projected.astype(jnp.bfloat16).reshape(
        image_count, windows_count, places, 3, HEADS, HEAD_DIM
    )
    queries = projected[:, :, :, 0]
    keys_part = projected[:, :, :, 1]
    values_part = projected[:, :, :, 2]

    def masked_scores():
        scores = (
            score_scale
            * jnp.einsum(
                "bnqhe,bnkhe->bnhqk", queries, keys_part, preferred_element_type=jnp.float32
            )
            + rel_bias
        )
        return jnp.where(allowed, scores, masked_score)

    masked = masked_scores()
    row_max = jnp.max(masked, axis=-1, keepdims=True)
    log_total = row_max + jnp.log(jnp.sum(jnp.exp(masked - row_max), axis=-1, keepdims=True))
    attention_low = jnp.exp(masked - log_total).astype(jnp.bfloat16)
    mixed_rows = jnp.einsum(
        "bnhqk,bnkhe->bnqhe", attention_low, values_part, preferred_element_type=jnp.float32
    )
    mixed_rows = mixed_rows.astype(jnp.bfloat16).reshape(row_count, D)
    attended = jnp.dot(mixed_rows, weight_proj, preferred_element_type=jnp.float32) + bias_proj
    resid_one = image_values + from_windows(attended.reshape(image_count, windows_count, places, D))
    normed_two, scaling_two = norm_stats(resid_one)
    input_two = (normed_two * gain_two + shift_two).astype(jnp.bfloat16).reshape(row_count, D)
    hidden_pre = jnp.dot(input_two, weight_up, preferred_element_type=jnp.float32) + bias_up
    hidden_act = jax.nn.gelu(hidden_pre, approximate=False).astype(jnp.bfloat16)
    result = resid_one + (
        jnp.dot(hidden_act, weight_down, preferred_element_type=jnp.float32) + bias_down
    ).reshape(image_count, SIDE, SIDE, D)
    output = result.astype(jnp.bfloat16)
    cot_rows = cotangent.reshape(row_count, D)
    grad_act = jnp.dot(cot_rows, weight_down.T, preferred_element_type=jnp.float32)
    down_grad = jnp.dot(hidden_act.T, cot_rows, preferred_element_type=jnp.float32)
    grad_pre = grad_act * gelu_slope(hidden_pre)
    pre_low = grad_pre.astype(jnp.bfloat16)
    up_grad = jnp.dot(input_two.T, pre_low, preferred_element_type=jnp.float32)
    grad_two = jnp.dot(pre_low, weight_up.T, preferred_element_type=jnp.float32).reshape(
        image_count, SIDE, SIDE, D
    )
    second_back, second_gain, second_shift = norm_back(grad_two, normed_two, scaling_two, gain_two)
    grad_resid = cotangent.astype(jnp.float32) + second_back
    grad_rows = to_windows(grad_resid.astype(jnp.bfloat16)).reshape(row_count, D)
    proj_grad = jnp.dot(mixed_rows.T, grad_rows, preferred_element_type=jnp.float32)
    mixed_grad = jnp.dot(grad_rows, weight_proj.T, preferred_element_type=jnp.float32).astype(
        jnp.bfloat16
    )
    mixed_grad = mixed_grad.reshape(image_count, windows_count, places, HEADS, HEAD_DIM)
    attention = jnp.exp(masked_scores() - log_total)
    attention_again = attention.astype(jnp.bfloat16)
    value_grad = jnp.einsum(
        "bnhqk,bnqhe->bnkhe", attention_again, mixed_grad, preferred_element_type=jnp.float32
    )
    prob_grad = jnp.einsum(
        "bnqhe,bnkhe->bnhqk", mixed_grad, values_part, preferred_element_type=jnp.float32
    )
    row_dot = jnp.sum(attention * prob_grad, axis=-1, keepdims=True)
    score_grad = attention * (prob_grad - row_dot)
    score_low = score_grad.astype(jnp.bfloat16)
    query_grad = score_scale * jnp.einsum(
        "bnhqk,bnkhe->bnqhe", score_low, keys_part, preferred_element_type=jnp.float32
    )
    key_grad = score_scale * jnp.einsum(
        "bnhqk,bnqhe->bnkhe", score_low, queries, preferred_element_type=jnp.float32
    )
    qkv_rows = (
        jnp.stack([query_grad, key_grad, value_grad], axis=3)
        .astype(jnp.bfloat16)
        .reshape(row_count, 3 * D)
    )
    qkv_grad = jnp.dot(window_rows.T, qkv_rows, preferred_element_type=jnp.float32)
    grad_one = from_windows(
        jnp.dot(qkv_rows, weight_qkv.T, preferred_element_type=jnp.float32).reshape(
            image_count, windows_count, places, D
        )
    )
    first_back, first_gain, first_shift = norm_back(grad_one, normed_one, scaling_one, gain_one)
    input_grad = (grad_resid + first_back).astype(jnp.bfloat16)
    rel_grad = jnp.sum(score_grad, axis=(0, 1)).transpose(1, 2, 0).reshape(places * places, HEADS)
    table_grad = jnp.dot(
        select_row.T, jnp.dot(select_offset.T, rel_grad, precision=highest), precision=highest
    )
    tokens_all = image_count * lax.axis_size("rep") * lax.axis_size("grp") * SIDE * SIDE
    grad_scale = 1.0 / math.sqrt(tokens_all)
    small_local = (
        jnp.concatenate(
            [
                first_gain,
                second_gain,
                first_shift,
                jnp.sum(query_grad, axis=(0, 1, 2)).reshape(D),
                jnp.sum(value_grad, axis=(0, 1, 2)).reshape(D),
                jnp.sum(grad_resid, axis=(0, 1, 2)),
                second_shift,
                jnp.sum(cot_rows, axis=0, dtype=jnp.float32),
                jnp.sum(grad_pre, axis=0),
                table_grad.reshape(-1),
            ]
        )
        * grad_scale
    )
    flat_grad = (
        jnp.concatenate(
            [
                qkv_grad.reshape(-1),
                proj_grad.reshape(-1),
                up_grad.reshape(-1),
                down_grad.reshape(-1),
            ]
        )
        * grad_scale
    )
    owned_grad = lax.psum_scatter(flat_grad, ("rep", "grp"), scatter_dimension=0, tiled=True)
    small_grad = lax.psum(small_local, ("rep", "grp"))
    new_matrices, new_matrix_m, new_matrix_v = adam_step(
        matrices, matrix_m, matrix_v, owned_grad, rate_matrix, decay_rate
    )
    new_small, new_small_m, new_small_v = adam_step(
        small, small_m, small_v, small_grad, rate_small, 0.0
    )
    return (
        output,
        input_grad,
        owned_grad,
        small_grad,
        new_matrices,
        new_matrix_m,
        new_matrix_v,
        new_small,
        new_small_m,
        new_small_v,
    )


def solution(mesh):
    in_specs = (
        P(("rep", "grp"), None, None, None),
        P(("rep", "grp"), None, None, None),
        P(),
        P(),
        P(("rep", "grp")),
        P(("rep", "grp")),
        P(("rep", "grp")),
        P(),
        P(),
        P(),
    )
    out_specs = (
        P(("rep", "grp"), None, None, None),
        P(("rep", "grp"), None, None, None),
        P(("rep", "grp")),
        P(),
        P(("rep", "grp")),
        P(("rep", "grp")),
        P(("rep", "grp")),
        P(),
        P(),
        P(),
    )
    return jax.shard_map(
        on_device, mesh=mesh, in_specs=in_specs, out_specs=out_specs, check_vma=False
    )
```

profile of v0, /device:TPU:0, one launch (start us, length us, event | category | flops | bytes accessed | tf_op | source)
XLA Modules:
  0.0 468.9 jit_solution(6778432741188791646)
XLA Ops:
  21.9 61.6 %all-gather.2.cloned.1.call-done = bf16[3145728]{0:T(1024)(128)(2,1)} async-done(((bf16[98304]{0:T(1024)(128)(2,1)}), bf16[3145728]{0:T(1024)(128)(2,1)}) %all-gather.2.cloned.1.call-update) | async-done | bytes 6291472 | tf_op jit(solution)/shard_map/all_gather | solution.py:131
  90.4 4.2 reshape.562
  94.6 3.1 fusion.71
  116.6 4.5 fusion.70
  121.1 4.4 slice.182
  128.3 2.8 convert_reduce_fusion
  132.7 4.6 slice.179
  137.3 6.9 %fusion.5 = (bf16[196,2048]{1,0:T(8,128)(2,1)S(1)}, f32[196,2048]{1,0:T(8,128)}) fusion(f32[2048]{0:T(1024)S(1)} %slice-done, bf16[196,512]{1,0:T(8,128)(2,1)} %reshape.543, bf16[512,2048]{1,0:T(8,128)(2,1)} %slice.179), kind=kOutput, calls=%fused_computation.20 | convolution fusion | flops 437534720 | bytes 4714496 | tf_op jit(solution)/shard_map/dot_general | solution.py:188
  148.7 3.3 fusion.74
  156.0 4.2 multiply_reduce_fusion.2
  160.2 3.9 fusion.65
  187.6 2.7 convolution_bitcast_fusion
  190.3 2.7 convolution_bitcast_fusion.1
  197.2 3.5 convert_element_type.105
  200.7 3.5 fusion.75
  204.2 4.5 reshape.550
  208.8 3.4 copy.139
  214.4 15.5 %maximum_multiply_fusion = f32[3145728]{0:T(1024)} fusion(f32[1048576]{0:T(1024)S(1)} %bitcast.114, f32[1048576]{0:T(1024)S(1)} %bitcast.115, f32[262144]{0:T(1024)S(1)} %bitcast.116, f32[786432]{0:T(1024)S(1)} %copy-done.1), kind=kLoop, calls=%fused_computation | loop fusion | flops 12582912 | bytes 25165824 | tf_op jit(solution)/shard_map/mul | solution.py:265
  229.9 2.7 reshape.558
  232.6 3.4 copy.125
  236.0 4.1 reshape.560
  245.1 5.4 %multiply_reduce_fusion.3 = (f32[512]{0:T(512)S(1)}, f32[14,14]{1,0:T(8,128)S(1)}, f32[14,14]{1,0:T(8,128)S(1)}, f32[1,14,14,512]{3,0,2,1:T(1,128)S(1)}) fusion(f32[14,14]{1,0:T(8,128)S(1)} %add_rsqrt_fusion.1, f32[14,14]{1,0:T(8,128)S(1)} %broadcast_multiply_fusion.6, bf16[1,14,14,512]{3,2,1,0:T(8,128)(2,1)S(1)} %copy-done.4, f32[512]{0:T(512)S(1)} %copy-done.36, ...), kind=kLoop, calls=%fused_computation.87 | loop fusion | flops 1002616 | bytes 1010752 | tf_op jit(solution)/shard_map/reduce_sum | solution.py:43
  252.8 41.0 %psum.7 = f32[8848]{0:T(1024)S(1)} all-reduce(f32[8848]{0:T(1024)S(1)} %broadcast_multiply_fusion.1), channel_id=1, replica_groups=mesh['rep'=8,'grp'=4] {'rep','grp'}, use_global_device_ids=true, to_apply=%region_23.24 | all-reduce | flops 8848 | bytes 70784 | tf_op jit(solution)/shard_map/psum | solution.py:276
  294.5 164.9 %all-reduce.3.cloned.1.call-done = f32[3145728]{0:T(1024)} async-done(((f32[3145728]{0:T(1024)}), f32[3145728]{0:T(1024)}) %all-reduce.3.cloned.1.call-update) | async-done | bytes 12582928
  (207 shorter events, 92.8 us)
Async XLA Ops:
  7.2 9.4 %slice-start.1 = ((f32[8848]{0:T(1024)}), f32[2704]{0:T(1024)S(1)}, s32[]{:S(2)}) async-start(f32[8848]{0:T(1024)} %param.17), calls=%async_computation.3 | async-start | bytes 24576 | tf_op jit(solution)/shard_map/slice | solution.py:114
  7.2 9.0 %copy-start.39 = (s32[14,14]{1,0:T(8,128)S(1)}, s32[14,14]{1,0:T(8,128)}, u32[]{:S(2)}) copy-start(s32[14,14]{1,0:T(8,128)} %param.12) | copy-start | bytes 2356
  7.2 9.5 %copy-start.26 = (bf16[1,14,14,512]{3,2,1,0:T(8,128)(2,1)S(1)}, bf16[1,14,14,512]{3,2,1,0:T(8,128)(2,1)}, u32[]{:S(2)}) copy-start(bf16[1,14,14,512]{3,2,1,0:T(8,128)(2,1)} %param.11) | copy-start | bytes 602116
  7.2 10.2 %copy-start.40 = (s32[169]{0:T(256)S(1)}, s32[169]{0:T(256)}, u32[]{:S(2)}) copy-start(s32[169]{0:T(256)} %param.13) | copy-start | bytes 2032
  7.2 76.3 %all-gather.2.cloned.1.call-start = ((), (), s32[]{:S(2)}) async-start(), calls=%async_computation | async-start | bytes 6488064 | tf_op jit(solution)/shard_map/all_gather | solution.py:131
  9.1 450.4 %all-reduce.3.cloned.1.call-start = ((), (), s32[]{:S(2)}) async-start(), calls=%async_computation.1 | async-start | bytes 25165824
  16.6 4.0 copy-start.37
  21.8 67.3 %copy-start.19 = (bf16[196,512]{1,0:T(8,128)(2,1)}, bf16[196,512]{1,0:T(8,128)(2,1)S(1)}, u32[]{:S(2)}) copy-start(bf16[196,512]{1,0:T(8,128)(2,1)S(1)} %reshape_reshape.10) | copy-start | bytes 602116
  121.1 7.2 %copy-start.32 = (f32[512]{0:T(512)S(1)}, f32[512]{0:T(512)}, u32[]{:S(2)}) copy-start(f32[512]{0:T(512)} %get-tuple-element.74) | copy-start | bytes 6148
  132.7 4.6 slice-start
  137.3 7.8 %copy-start.18 = (bf16[2048,512]{1,0:T(8,128)(2,1)S(1)}, bf16[2048,512]{1,0:T(8,128)(2,1)}, u32[]{:S(2)}) copy-start(bf16[2048,512]{1,0:T(8,128)(2,1)} %slice.182) | copy-start | bytes 6291460
  137.3 7.8 %copy-start.42 = (f32[512]{0:T(512)S(1)}, f32[512]{0:T(512)}, u32[]{:S(2)}) copy-start(f32[512]{0:T(512)} %get-tuple-element.72) | copy-start | bytes 6148
  148.7 3.3 copy-start.3
  197.2 3.5 copy-start.20
  208.7 3.5 copy-start
  236.0 4.1 copy-start.23
  242.9 7.6 %copy-start.13 = (f32[1,14,14,512]{3,0,2,1:T(1,128)S(1)}, f32[1,14,14,512]{3,0,2,1:T(1,128)}, u32[]{:S(2)}) copy-start(f32[1,14,14,512]{3,0,2,1:T(1,128)} %copy-done.12) | copy-start | bytes 1204228
  245.0 48.8 %copy-start.30 = (f32[8848]{0:T(1024)S(1)}, f32[8848]{0:T(1024)}, u32[]{:S(2)}) copy-start(f32[8848]{0:T(1024)} %param.17) | copy-start | bytes 106180
  245.0 48.8 %copy-start.33 = (f32[8848]{0:T(1024)S(1)}, f32[8848]{0:T(1024)}, u32[]{:S(2)}) copy-start(f32[8848]{0:T(1024)} %param.18) | copy-start | bytes 106180
  245.0 48.8 %copy-start.34 = (f32[8848]{0:T(1024)S(1)}, f32[8848]{0:T(1024)}, u32[]{:S(2)}) copy-start(f32[8848]{0:T(1024)} %param.19) | copy-start | bytes 106180
  245.1 214.4 %copy-start.24 = (f32[98304]{0:T(1024)S(1)}, f32[98304]{0:T(1024)}, u32[]{:S(2)}) copy-start(f32[98304]{0:T(1024)} %param.14) | copy-start | bytes 1179652
  245.1 214.3 %copy-start.28 = (f32[98304]{0:T(1024)S(1)}, f32[98304]{0:T(1024)}, u32[]{:S(2)}) copy-start(f32[98304]{0:T(1024)} %param.15) | copy-start | bytes 1179652
  245.1 214.3 %copy-start.29 = (f32[98304]{0:T(1024)S(1)}, f32[98304]{0:T(1024)}, u32[]{:S(2)}) copy-start(f32[98304]{0:T(1024)} %param.16) | copy-start | bytes 1179652
  293.8 167.8 %copy-start.31 = (f32[8848]{0:T(1024)}, f32[8848]{0:T(1024)S(1)}, u32[]{:S(2)}) copy-start(f32[8848]{0:T(1024)S(1)} %psum.7) | copy-start | bytes 106180
  (23 other events, 40.6 us)
Sparse Core Ops, SparseCore 0:
  11.5 71.9 all-gather.1
  230.0 229.3 all-reduce.2
where the time goes:
time: 477 us; the launch traced here: 469 us
  waiting for transfers between devices  227 us (48%)
  local copies, waits for them, and re-layouts  93.5 us (20%)
  other arithmetic  52.5 us (11%)
  blocking collectives  41 us (9%)
  matrix products  39.9 us (8%)
  between operations  15.4 us (3%)
    unnamed x3, waiting for transfers between devices  165 us
    all_gather x1, waiting for transfers between devices, on_device(): gathered = lax.all_gather(low_shard, ('rep', 'grp'), axis=0, tiled=True)  61.6 us
    psum x1, blocking collectives, on_device(): small_grad = lax.psum(small_local, ('rep', 'grp'))  41 us
    unnamed x102, local copies, waits for them, and re-layouts  16.9 us
    mul x1, other arithmetic, on_device(): jnp.concatenate([qkv_grad.reshape(-1), proj_grad.reshape(-1), up_grad.res...  15.5 us
    convert_element_type x4, local copies, waits for them, and re-layouts, on_device(): qkv_rows = jnp.stack([query_grad, key_grad, value_grad], axis=3).astype(j...  13.5 us
    reduce_sum x2, other arithmetic, norm_back(): jnp.sum(incoming * normed, axis=(0, 1, 2))  9.56 us
  transfers between devices with their start and end apart: 2, of which 2 were waited for; matrix products, arithmetic and copies ran while one was open for 8% of the time, Pallas kernels for 0%

commit v1 on v0

--- a/solution.py
+++ b/solution.py
@@ -273,7 +273,7 @@
         * grad_scale
     )
     owned_grad = lax.psum_scatter(flat_grad, ("rep", "grp"), scatter_dimension=0, tiled=True)
-    small_grad = lax.psum(small_local, ("rep", "grp"))
+    small_grad = jnp.sum(lax.all_gather(small_local, ("rep", "grp")), axis=0)
     new_matrices, new_matrix_m, new_matrix_v = adam_step(
         matrices, matrix_m, matrix_v, owned_grad, rate_matrix, decay_rate
     )

time: 477 us -> 507 us (1.063)
  waiting for transfers between devices: 227 us -> 318 us
  blocking collectives: 41 us -> 0 us
  local copies, waits for them, and re-layouts: 93.5 us -> 75 us
    unnamed x3 -> x4, waiting for transfers between devices: 165 us -> 233 us
    psum x1 -> x0, blocking collectives: 41 us -> none  [on_device(): small_grad = lax.psum(small_local, ('rep', 'grp'))]
    all_gather x0 -> x1, waiting for transfers between devices: none -> 23.1 us  [on_device(): small_grad = jnp.sum(lax.all_gather(small_local, ('rep', 'grp')), axis=0)]
    unnamed x102 -> x111, local copies, waits for them, and re-layouts: 16.9 us -> 16 us
  transfers between devices with their start and end apart: 2 -> 3, of which waited for: 2 -> 3; matrix products, arithmetic and copies ran while one was open for 8% -> 9% of each run, Pallas kernels for 0% -> 0%
where the time goes in v1:
time: 507 us; the launch traced here: 498 us
  waiting for transfers between devices  318 us (63%)
  local copies, waits for them, and re-layouts  75 us (15%)
  other arithmetic  54.9 us (11%)
  matrix products  35.1 us (7%)
  between operations  15.1 us (3%)
    unnamed x4, waiting for transfers between devices  233 us
    all_gather x1, waiting for transfers between devices, on_device(): gathered = lax.all_gather(low_shard, ('rep', 'grp'), axis=0, tiled=True)  62.2 us
    all_gather x1, waiting for transfers between devices, on_device(): small_grad = jnp.sum(lax.all_gather(small_local, ('rep', 'grp')), axis=0)  23.1 us
    unnamed x111, local copies, waits for them, and re-layouts  16 us
    mul x1, other arithmetic, on_device(): jnp.concatenate([qkv_grad.reshape(-1), proj_grad.reshape(-1), up_grad.res...  15.5 us
    convert_element_type x4, local copies, waits for them, and re-layouts, on_device(): qkv_rows = jnp.stack([query_grad, key_grad, value_grad], axis=3).astype(j...  10.3 us
  transfers between devices with their start and end apart: 3, of which 3 were waited for; matrix products, arithmetic and copies ran while one was open for 9% of the time, Pallas kernels for 0%

profile of v1, /device:TPU:0, one launch (start us, length us, event | category | flops | bytes accessed | tf_op | source)
XLA Modules:
  0.0 498.2 jit_solution(9530544378631424900)
XLA Ops:
  21.3 62.2 %all-gather.4.cloned.1.call-done = bf16[3145728]{0:T(1024)(128)(2,1)} async-done(((bf16[98304]{0:T(1024)(128)(2,1)}), bf16[3145728]{0:T(1024)(128)(2,1)}) %all-gather.4.cloned.1.call-update) | async-done | bytes 6291472 | tf_op jit(solution)/shard_map/all_gather | solution.py:131
  85.0 2.7 reshape.687
  93.0 3.2 reshape.691
  109.2 4.5 fusion.70
  113.7 4.4 slice.182
  122.9 4.6 slice.179
  127.5 6.8 %fusion.5 = (bf16[196,2048]{1,0:T(8,128)(2,1)S(1)}, f32[196,2048]{1,0:T(8,128)}) fusion(f32[2048]{0:T(1024)S(1)} %slice-done, bf16[196,512]{1,0:T(8,128)(2,1)S(1)} %reshape.673, bf16[512,2048]{1,0:T(8,128)(2,1)} %slice.179), kind=kOutput, calls=%fused_computation.20 | convolution fusion | flops 437534720 | bytes 4714496 | tf_op jit(solution)/shard_map/dot_general | solution.py:188
  136.6 2.3 reshape.688
  138.8 3.3 fusion.74
  143.8 2.3 reshape.692
  146.0 4.1 multiply_reduce_fusion.2
  150.1 5.0 %fusion.65 = (f32[512]{0:T(512)}, f32[1,14,14,512]{3,0,2,1:T(1,128)S(1)}, bf16[1,14,14,512]{3,0,2,1:T(2,128)(2,1)}, f32[512]{0:T(512)}) fusion(f32[14,14]{1,0:T(8,128)S(1)} %broadcast_multiply_fusion.3, f32[1,14,14,512]{3,0,2,1:T(1,128)S(1)} %get-tuple-element.64, f32[14,14]{1,0:T(8,128)S(1)} %broadcast_multiply_fusion.4, f32[14,14]{1,0:T(8,128)S(1)} %div.78, ...), kind=kLoop, calls=%fused_computation.154 | loop fusion | flops 1303552 | bytes 2016320 | tf_op jit(solution)/shard_map/reduce_sum | solution.py:255
  173.4 3.4 copy.125
  176.8 4.8 reshape.689
  184.8 2.7 convolution_bitcast_fusion
  187.5 2.7 convolution_bitcast_fusion.1
  194.4 5.9 %multiply_reduce_fusion.3 = (f32[512]{0:T(512)S(1)}, f32[14,14]{1,0:T(8,128)S(1)}, f32[14,14]{1,0:T(8,128)S(1)}, f32[1,14,14,512]{3,0,2,1:T(1,128)}) fusion(f32[14,14]{1,0:T(8,128)S(1)} %add_rsqrt_fusion.1, f32[14,14]{1,0:T(8,128)S(1)} %broadcast_multiply_fusion.5, bf16[1,14,14,512]{3,2,1,0:T(8,128)(2,1)S(1)} %copy-done.2, f32[512]{0:T(512)S(1)} %get-tuple-element.79, ...), kind=kLoop, calls=%fused_computation.87 | loop fusion | flops 1002616 | bytes 1010752 | tf_op jit(solution)/shard_map/reduce_sum | solution.py:43
  201.2 2.4 fusion.75
  203.6 2.9 reshape.680
  206.5 3.5 copy.139
  211.2 15.5 %maximum_multiply_fusion = f32[3145728]{0:T(1024)} fusion(f32[1048576]{0:T(1024)S(1)} %bitcast.123, f32[1048576]{0:T(1024)S(1)} %bitcast.124, f32[262144]{0:T(1024)S(1)} %bitcast.125, f32[786432]{0:T(1024)S(1)} %reshape.680), kind=kLoop, calls=%fused_computation | loop fusion | flops 12582912 | bytes 25165824 | tf_op jit(solution)/shard_map/mul | solution.py:265
  230.7 23.1 %all-gather.6.cloned.1.call-done = f32[32,1,8848]{2,1,0:T(1,128)} async-done(((f32[1,1,8848]{2,1,0:T(1,128)}), f32[32,1,8848]{2,1,0:T(1,128)}) %all-gather.6.cloned.1.call-update) | async-done | bytes 1132560 | tf_op jit(solution)/shard_map/all_gather | solution.py:276
  256.4 232.6 %all-reduce.3.cloned.1.call-done = f32[3145728]{0:T(1024)} async-done(((f32[3145728]{0:T(1024)}), f32[3145728]{0:T(1024)}) %all-reduce.3.cloned.1.call-update) | async-done | bytes 12582928
  489.0 2.2 multiply_subtract_fusion
  (218 shorter events, 76.2 us)
Async XLA Ops:
  7.2 8.8 %slice-start.1 = ((f32[8848]{0:T(1024)}), f32[2704]{0:T(1024)S(1)}, s32[]{:S(2)}) async-start(f32[8848]{0:T(1024)} %param.17), calls=%async_computation.4 | async-start | bytes 24576 | tf_op jit(solution)/shard_map/slice | solution.py:114
  7.2 8.4 %copy-start.42 = (s32[14,14]{1,0:T(8,128)S(1)}, s32[14,14]{1,0:T(8,128)}, u32[]{:S(2)}) copy-start(s32[14,14]{1,0:T(8,128)} %param.12) | copy-start | bytes 2356
  7.2 8.9 %copy-start.31 = (bf16[1,14,14,512]{3,2,1,0:T(8,128)(2,1)S(1)}, bf16[1,14,14,512]{3,2,1,0:T(8,128)(2,1)}, u32[]{:S(2)}) copy-start(bf16[1,14,14,512]{3,2,1,0:T(8,128)(2,1)} %param.11) | copy-start | bytes 602116
  7.2 9.6 %copy-start.45 = (s32[169]{0:T(256)S(1)}, s32[169]{0:T(256)}, u32[]{:S(2)}) copy-start(s32[169]{0:T(256)} %param.13) | copy-start | bytes 2032
  7.2 76.3 %all-gather.4.cloned.1.call-start = ((), (), s32[]{:S(2)}) async-start(), calls=%async_computation | async-start | bytes 6488064 | tf_op jit(solution)/shard_map/all_gather | solution.py:131
  9.1 244.7 %all-gather.6.cloned.1.call-start = ((), (), s32[]{:S(2)}) async-start(), calls=%async_computation.1 | async-start | bytes 1182720 | tf_op jit(solution)/shard_map/all_gather | solution.py:276
  21.2 70.5 %copy-start.22 = (bf16[196,512]{1,0:T(8,128)(2,1)}, bf16[196,512]{1,0:T(8,128)(2,1)S(1)}, u32[]{:S(2)}) copy-start(bf16[196,512]{1,0:T(8,128)(2,1)S(1)} %reshape_reshape.10) | copy-start | bytes 602116
  99.7 4.7 copy-start.6
  122.8 4.7 copy-start.29
  127.5 7.7 %copy-start.21 = (bf16[2048,512]{1,0:T(8,128)(2,1)S(1)}, bf16[2048,512]{1,0:T(8,128)(2,1)}, u32[]{:S(2)}) copy-start(bf16[2048,512]{1,0:T(8,128)(2,1)} %slice.182) | copy-start | bytes 6291460
  143.7 6.4 %copy-start.32 = (bf16[1,14,14,512]{3,2,1,0:T(8,128)(2,1)S(1)}, bf16[1,14,14,512]{3,2,1,0:T(8,128)(2,1)}, u32[]{:S(2)}) copy-start(bf16[1,14,14,512]{3,2,1,0:T(8,128)(2,1)} %param.11) | copy-start | bytes 602116
  157.1 5.4 %copy-start.20 = (bf16[196,512]{0,1:T(8,128)(2,1)S(1)}, bf16[196,512]{0,1:T(8,128)(2,1)}, u32[]{:S(2)}) copy-start(bf16[196,512]{0,1:T(8,128)(2,1)} %copy-done.19) | copy-start | bytes 602116
  176.8 4.8 copy-start.27
  193.5 6.9 %copy-start.44 = (f32[512]{0:T(512)S(1)}, f32[512]{0:T(512)}, u32[]{:S(2)}) copy-start(f32[512]{0:T(512)} %get-tuple-element.56) | copy-start | bytes 6148
  193.5 6.9 %copy-start.43 = (f32[512]{0:T(512)S(1)}, f32[512]{0:T(512)}, u32[]{:S(2)}) copy-start(f32[512]{0:T(512)} %get-tuple-element.71) | copy-start | bytes 6148
  193.5 7.7 %copy-start.23 = (bf16[196,512]{1,0:T(8,128)(2,1)S(1)}, bf16[196,512]{1,0:T(8,128)(2,1)}, u32[]{:S(2)}) copy-start(bf16[196,512]{1,0:T(8,128)(2,1)} %copy-done.22) | copy-start | bytes 602116
  201.2 287.8 %all-reduce.3.cloned.1.call-start = ((), (), s32[]{:S(2)}) async-start(), calls=%async_computation.2 | async-start | bytes 25165824
  228.4 27.2 %copy-start.39 = (f32[8848]{0:T(1024)S(1)}, f32[8848]{0:T(1024)}, u32[]{:S(2)}) copy-start(f32[8848]{0:T(1024)} %param.17) | copy-start | bytes 106180
  228.4 27.2 %copy-start.40 = (f32[8848]{0:T(1024)S(1)}, f32[8848]{0:T(1024)}, u32[]{:S(2)}) copy-start(f32[8848]{0:T(1024)} %param.18) | copy-start | bytes 106180
  228.5 27.2 %copy-start.41 = (f32[8848]{0:T(1024)S(1)}, f32[8848]{0:T(1024)}, u32[]{:S(2)}) copy-start(f32[8848]{0:T(1024)} %param.19) | copy-start | bytes 106180
  228.5 260.5 %copy-start.28 = (f32[98304]{0:T(1024)S(1)}, f32[98304]{0:T(1024)}, u32[]{:S(2)}) copy-start(f32[98304]{0:T(1024)} %param.14) | copy-start | bytes 1179652
  228.5 260.5 %copy-start.36 = (f32[98304]{0:T(1024)S(1)}, f32[98304]{0:T(1024)}, u32[]{:S(2)}) copy-start(f32[98304]{0:T(1024)} %param.15) | copy-start | bytes 1179652
  228.5 260.5 %copy-start.37 = (f32[98304]{0:T(1024)S(1)}, f32[98304]{0:T(1024)}, u32[]{:S(2)}) copy-start(f32[98304]{0:T(1024)} %param.16) | copy-start | bytes 1179652
  255.7 235.5 %copy-start.38 = (f32[8848]{0:T(1024)}, f32[8848]{0:T(1024)S(1)}, u32[]{:S(2)}) copy-start(f32[8848]{0:T(1024)S(1)} %reduce_sum.225) | copy-start | bytes 106180
  (28 other events, 60.0 us)
Sparse Core Ops, SparseCore 0:
  11.5 71.9 all-gather.3
  201.3 52.4 all-gather.5
  259.8 229.1 all-reduce.2
